TPU v7x, 32 devices: a whole 2x2x4 slice. The times are simulated.
32 devices in a mesh: req: 2 (over y), tm: 4 (over z), rows: 2 (over x), sub: 2 (over core).
Axes of the slice: x: 2, y: 2, z: 4, core: 2. Of those that a mesh axis runs over, the one named last changes fastest.
Arguments:
- latents: bfloat16 [32, 256, 640], P('tm', ('req', 'rows')), parts along dimension 1, may hold values from -6 to 6
- cotangent: bfloat16 [32, 256, 640], P('tm', ('req', 'rows')), parts along dimension 1, may hold values from -6 to 6
- w_qkv: bfloat16 [640, 3, 640], P(None, None, 'sub'), may hold values from -0.25 to 0.25
- w_out: bfloat16 [640, 640], P('sub'), may hold values from -0.25 to 0.25
- time_bias: float32 [8, 63], replicated, may hold values from -4 to 310
Outputs:
- grad_latents: bfloat16 [32, 256, 640], P('tm', ('req', 'rows'), 'sub'), parts along dimension 1
- grad_w_qkv: float32 [1280, 3, 640], P(('req', 'tm', 'rows'), None, 'sub'), parts along dimension 0
- grad_w_out_t: float32 [1280, 640], P(('req', 'tm', 'rows'), 'sub'), parts along dimension 0
There are 2 independent parts, one for each index of `req`. A program takes and returns all parts, laid end to end along the dimension named above; an argument that names none is the same for every part. Nothing has to cross between parts.
All inputs are finite; a program needn't handle non-finite values.
Results may differ from a plain program's by a relative error of at most 0.012.
Values may be sent and summed in bfloat16 or wider, within the bound.
No kernel may reach another device: no remote copies, remote signals or barrier semaphores. Data moves between devices by JAX's collectives and lax.ppermute only.
A program may use at most 128 MiB of HBM per device.

v0:
```python
import math
import jax
import jax.numpy as jnp
from jax import lax
from jax.sharding import PartitionSpec as P

H = 8


def positional(frame_pos, channels):
    half = channels // 2
    frequency = jnp.exp(-math.log(10000.0) * jnp.arange(half, dtype=jnp.float32) * 2.0 / channels)
    angles = frame_pos.astype(jnp.float32)[:, None] * frequency[None, :]
    return jnp.concatenate((jnp.sin(angles), jnp.cos(angles)), axis=1)


def bias_table(bias_rows, frames):
    offsets = (
        jnp.arange(frames, dtype=jnp.int32)[:, None]
        - jnp.arange(frames, dtype=jnp.int32)[None, :]
        + frames
        - 1
    )
    return bias_rows[:, offsets]


def embed(latents, frame_pos):
    return (
        latents.astype(jnp.float32) + positional(frame_pos, latents.shape[2])[:, None, :]
    ).astype(jnp.bfloat16)


def project(hidden, w_qkv, cotangent, w_out):
    qkv = jnp.einsum("fsc,ctd->fstd", hidden, w_qkv, preferred_element_type=jnp.float32).astype(
        jnp.bfloat16
    )
    grad_attn = jnp.einsum(
        "fse,de->fsd", cotangent, w_out, preferred_element_type=jnp.float32
    ).astype(jnp.bfloat16)
    return (qkv[:, :, 0], qkv[:, :, 1], qkv[:, :, 2], grad_attn)


def attend(query_rows, key_rows, value_rows, grad_rows, bias_rows, head_count):
    frames, positions, local_width = query_rows.shape
    head_size = local_width // head_count
    inv_root = 1.0 / math.sqrt(head_size)
    shape4 = (frames, positions, head_count, head_size)
    query_heads = query_rows.reshape(shape4)
    key_heads = key_rows.reshape(shape4)
    value_heads = value_rows.reshape(shape4)
    grad_heads = grad_rows.reshape(shape4)
    scores = (
        jnp.einsum("iphd,jphd->phij", query_heads, key_heads, preferred_element_type=jnp.float32)
        * inv_root
        + bias_rows[None]
    )
    row_max = jnp.max(scores, axis=-1, keepdims=True)
    raw_weights = jnp.exp(scores - row_max)
    probs = raw_weights / jnp.sum(raw_weights, axis=-1, keepdims=True)
    probs_low = probs.astype(jnp.bfloat16)
    attn_out = jnp.einsum(
        "phij,jphd->iphd", probs_low, value_heads, preferred_element_type=jnp.float32
    ).astype(jnp.bfloat16)
    grad_probs = jnp.einsum(
        "iphd,jphd->phij", grad_heads, value_heads, preferred_element_type=jnp.float32
    )
    row_dot = jnp.sum(probs * grad_probs, axis=-1, keepdims=True)
    grad_scores = (probs * (grad_probs - row_dot) * inv_root).astype(jnp.bfloat16)
    grad_query = jnp.einsum(
        "phij,jphd->iphd", grad_scores, key_heads, preferred_element_type=jnp.float32
    ).astype(jnp.bfloat16)
    grad_key = jnp.einsum(
        "phij,iphd->jphd", grad_scores, query_heads, preferred_element_type=jnp.float32
    ).astype(jnp.bfloat16)
    grad_value = jnp.einsum(
        "phij,iphd->jphd", probs_low, grad_heads, preferred_element_type=jnp.float32
    ).astype(jnp.bfloat16)
    flat = (frames, positions, local_width)
    return (
        attn_out.reshape(flat),
        grad_query.reshape(flat),
        grad_key.reshape(flat),
        grad_value.reshape(flat),
    )


def latent_grad(grad_qkv, w_qkv, cotangent, head_group):
    local_width = w_qkv.shape[2]
    back_term = jnp.einsum("fstd,ctd->fsc", grad_qkv, w_qkv, preferred_element_type=jnp.float32)
    summed_back = lax.psum_scatter(
        back_term.astype(jnp.bfloat16), "sub", scatter_dimension=2, tiled=True
    ).astype(jnp.float32)
    own_cotangent = lax.dynamic_slice_in_dim(cotangent, head_group * local_width, local_width, 2)
    return (own_cotangent.astype(jnp.float32) + summed_back).astype(jnp.bfloat16)


def per_device(latents, cotangent, w_qkv, w_out, time_bias):
    channels = latents.shape[2]
    local_width = w_qkv.shape[2]
    head_count = H // lax.axis_size("sub")
    head_group = lax.axis_index("sub")
    all_frames = latents.shape[0] * lax.axis_size("tm")
    bias_rows = bias_table(
        lax.dynamic_slice_in_dim(time_bias, head_group * head_count, head_count, 0), all_frames
    )
    frame_pos = lax.axis_index("tm") * latents.shape[0] + jnp.arange(
        latents.shape[0], dtype=jnp.int32
    )
    hidden = embed(latents, frame_pos)
    query_rows, key_rows, value_rows, grad_attn = project(hidden, w_qkv, cotangent, w_out)
    query_rows, key_rows, value_rows, grad_attn = (
        lax.all_to_all(query_rows, "tm", split_axis=1, concat_axis=0, tiled=True),
        lax.all_to_all(key_rows, "tm", split_axis=1, concat_axis=0, tiled=True),
        lax.all_to_all(value_rows, "tm", split_axis=1, concat_axis=0, tiled=True),
        lax.all_to_all(grad_attn, "tm", split_axis=1, concat_axis=0, tiled=True),
    )
    attn_out, grad_query, grad_key, grad_value = attend(
        query_rows, key_rows, value_rows, grad_attn, bias_rows, head_count
    )
    attn_out, grad_query, grad_key, grad_value = (
        lax.all_to_all(attn_out, "tm", split_axis=0, concat_axis=1, tiled=True),
        lax.all_to_all(grad_query, "tm", split_axis=0, concat_axis=1, tiled=True),
        lax.all_to_all(grad_key, "tm", split_axis=0, concat_axis=1, tiled=True),
        lax.all_to_all(grad_value, "tm", split_axis=0, concat_axis=1, tiled=True),
    )
    grad_qkv = jnp.stack((grad_query, grad_key, grad_value), axis=2)
    grad_latents = latent_grad(grad_qkv, w_qkv, cotangent, head_group)
    flat_hidden = hidden.reshape(-1, channels)
    flat_cotangent = cotangent.reshape(-1, channels)
    flat_grads = grad_qkv.reshape(-1, 3 * local_width)
    flat_out = attn_out.reshape(-1, local_width)
    qkv_part = lax.dot_general(
        flat_hidden, flat_grads, (((0,), (0,)), ((), ())), preferred_element_type=jnp.float32
    )
    out_part = lax.dot_general(
        flat_cotangent, flat_out, (((0,), (0,)), ((), ())), preferred_element_type=jnp.float32
    )
    summed_grads = lax.psum_scatter(
        jnp.concatenate((qkv_part, out_part), axis=1),
        ("tm", "rows"),
        scatter_dimension=0,
        tiled=True,
    )
    grad_w_qkv = summed_grads[:, : 3 * local_width].reshape(-1, 3, local_width)
    grad_w_out_t = summed_grads[:, 3 * local_width :]
    return (grad_latents, grad_w_qkv, grad_w_out_t)


def solution(mesh):
    return jax.shard_map(
        per_device,
        mesh=mesh,
        in_specs=(
            P("tm", ("req", "rows"), None),
            P("tm", ("req", "rows"), None),
            P(None, None, "sub"),
            P("sub", None),
            P(),
        ),
        out_specs=(
            P("tm", ("req", "rows"), "sub"),
            P(("req", "tm", "rows"), None, "sub"),
            P(("req", "tm", "rows"), "sub"),
        ),
        check_vma=False,
    )
```

profile of v0, /device:TPU:0, one launch (start us, length us, event | category | flops | bytes accessed | tf_op | source)
XLA Modules:
  0.0 233.2 jit_solution(9928908016868254245)
XLA Ops:
  10.0 6.3 %all-to-all-start.2 = ((bf16[8,64,320]{2,0,1:T(8,128)(2,1)}), bf16[8,64,320]{2,0,1:T(8,128)(2,1)S(1)}, u32[]{:S(2)}, u32[]{:S(2)}) async-start(bf16[8,64,320]{2,0,1:T(8,128)(2,1)} %copy.49), calls=%async_computation.2 | async-start | bytes 786432 | tf_op jit(solution)/shard_map/all_to_all | solution.py:115
  19.0 9.0 %all-to-all-done.2 = bf16[8,64,320]{2,0,1:T(8,128)(2,1)S(1)} async-done(((bf16[8,64,320]{2,0,1:T(8,128)(2,1)}), bf16[8,64,320]{2,0,1:T(8,128)(2,1)S(1)}, u32[]{:S(2)}, u32[]{:S(2)}) %all-to-all-start.2) | async-done | bytes 327712 | tf_op jit(solution)/shard_map/all_to_all | solution.py:115
  28.1 3.5 %all-to-all-start.3 = ((bf16[8,64,320]{2,0,1:T(8,128)(2,1)}), bf16[8,64,320]{2,0,1:T(8,128)(2,1)S(1)}, u32[]{:S(2)}, u32[]{:S(2)}) async-start(bf16[8,64,320]{2,0,1:T(8,128)(2,1)} %copy.51), calls=%async_computation.3 | async-start | bytes 786432 | tf_op jit(solution)/shard_map/all_to_all | solution.py:114
  32.5 9.9 %all-to-all-done.3 = bf16[8,64,320]{2,0,1:T(8,128)(2,1)S(1)} async-done(((bf16[8,64,320]{2,0,1:T(8,128)(2,1)}), bf16[8,64,320]{2,0,1:T(8,128)(2,1)S(1)}, u32[]{:S(2)}, u32[]{:S(2)}) %all-to-all-start.3) | async-done | bytes 327712 | tf_op jit(solution)/shard_map/all_to_all | solution.py:114
  42.4 3.5 %all-to-all-start.1 = ((bf16[8,64,320]{2,0,1:T(8,128)(2,1)}), bf16[8,64,320]{2,0,1:T(8,128)(2,1)S(1)}, u32[]{:S(2)}, u32[]{:S(2)}) async-start(bf16[8,64,320]{2,0,1:T(8,128)(2,1)} %copy.43), calls=%async_computation.1 | async-start | bytes 786432 | tf_op jit(solution)/shard_map/all_to_all | solution.py:112
  46.8 8.8 %all-to-all-done.1 = bf16[8,64,320]{2,0,1:T(8,128)(2,1)S(1)} async-done(((bf16[8,64,320]{2,0,1:T(8,128)(2,1)}), bf16[8,64,320]{2,0,1:T(8,128)(2,1)S(1)}, u32[]{:S(2)}, u32[]{:S(2)}) %all-to-all-start.1) | async-done | bytes 327712 | tf_op jit(solution)/shard_map/all_to_all | solution.py:112
  55.7 3.5 %all-to-all-start = ((bf16[8,64,320]{2,0,1:T(8,128)(2,1)}), bf16[8,64,320]{2,0,1:T(8,128)(2,1)S(1)}, u32[]{:S(2)}, u32[]{:S(2)}) async-start(bf16[8,64,320]{2,0,1:T(8,128)(2,1)} %copy.41), calls=%async_computation | async-start | bytes 786432 | tf_op jit(solution)/shard_map/all_to_all | solution.py:113
  59.4 4.0 %gather_fusion = f32[1024,4]{1,0:T(8,128)} fusion(f32[4,63]{0,1:T(8,128)S(1)} %copy.80, s32[1024]{0:T(1024)S(1)} %broadcast_clamp_fusion), kind=kCustom, calls=%fused_computation | custom fusion | bytes 36864 | tf_op jit(solution)/shard_map/gather | solution.py:24
  65.5 2.1 reshape.98
  73.8 2.5 %fusion.13 = bf16[32,16,4,80]{3,0,2,1:T(8,128)(2,1)} fusion(bf16[32,16,4,80]{3,2,1,0:T(4,128)(2,1)} %reshape.98, f32[16,4,32]{2,1,0:T(4,128)S(1)} %get-tuple-element.17, f32[16,4,32,32]{2,3,1,0:T(8,128)S(1)} %fusion.7), kind=kOutput, calls=%fused_computation.25 | convolution fusion | flops 10848287 | bytes 925696 | tf_op jit(solution)/shard_map/phij,iphd->jphd/dot_general | solution.py:75
  78.7 5.0 %all-to-all-start.6 = ((bf16[32,16,320]{2,1,0:T(8,128)(2,1)}), bf16[32,16,320]{2,1,0:T(8,128)(2,1)}, u32[]{:S(2)}, u32[]{:S(2)}) async-start(bf16[32,16,320]{2,1,0:T(8,128)(2,1)} %reshape.102), calls=%async_computation.6 | async-start | bytes 786432 | tf_op jit(solution)/shard_map/all_to_all | solution.py:124
  83.7 3.0 %fusion.27 = f32[16,4,32,32]{2,3,1,0:T(8,128)} fusion(bf16[32,16,4,80]{3,2,1,0:T(4,128)(2,1)} %reshape.99, bf16[32,16,4,80]{3,2,1,0:T(4,128)(2,1)} %reshape.98), kind=kOutput, calls=%fused_computation.39 | convolution fusion | flops 10485760 | bytes 917504 | tf_op jit(solution)/shard_map/iphd,jphd->phij/dot_general | solution.py:64
  86.7 3.7 %fusion.12 = bf16[32,16,4,80]{3,0,2,1:T(8,128)(2,1)} fusion(f32[16,4,32,32]{2,3,1,0:T(8,128)} %fusion.27, bf16[32,16,4,80]{3,2,1,0:T(4,128)(2,1)S(1)} %copy-done.3, f32[16,4,32,32]{2,3,1,0:T(8,128)} %get-tuple-element.18, f32[16,4,32]{2,1,0:T(4,128)S(1)} %get-tuple-element.17), kind=kOutput, calls=%fused_computation.24 | convolution fusion | flops 11110431 | bytes 1187840 | tf_op jit(solution)/shard_map/phij,iphd->jphd/dot_general | solution.py:72
  93.0 5.0 %all-to-all-start.5 = ((bf16[32,16,320]{2,1,0:T(8,128)(2,1)}), bf16[32,16,320]{2,1,0:T(8,128)(2,1)}, u32[]{:S(2)}, u32[]{:S(2)}) async-start(bf16[32,16,320]{2,1,0:T(8,128)(2,1)} %reshape.101), calls=%async_computation.5 | async-start | bytes 786432 | tf_op jit(solution)/shard_map/all_to_all | solution.py:123
  98.0 3.9 %fusion.10 = bf16[32,16,4,80]{3,0,2,1:T(8,128)(2,1)} fusion(f32[16,4,32,32]{2,3,1,0:T(8,128)} %fusion.27, bf16[32,16,4,80]{3,2,1,0:T(4,128)(2,1)} %copy-done.2, f32[16,4,32,32]{2,3,1,0:T(8,128)} %get-tuple-element.18, f32[16,4,32]{2,1,0:T(4,128)S(1)} %get-tuple-element.17), kind=kOutput, calls=%fused_computation.22 | convolution fusion | flops 11110431 | bytes 1187840 | tf_op jit(solution)/shard_map/phij,jphd->iphd/dot_general | solution.py:69
  104.3 2.7 %all-to-all-done.5 = bf16[32,16,320]{2,1,0:T(8,128)(2,1)} async-done(((bf16[32,16,320]{2,1,0:T(8,128)(2,1)}), bf16[32,16,320]{2,1,0:T(8,128)(2,1)}, u32[]{:S(2)}, u32[]{:S(2)}) %all-to-all-start.5) | async-done | bytes 327712 | tf_op jit(solution)/shard_map/all_to_all | solution.py:123
  107.0 3.6 %all-to-all-start.4 = ((bf16[32,16,320]{2,1,0:T(8,128)(2,1)}), bf16[32,16,320]{2,1,0:T(8,128)(2,1)S(1)}, u32[]{:S(2)}, u32[]{:S(2)}) async-start(bf16[32,16,320]{2,1,0:T(8,128)(2,1)} %reshape.100), calls=%async_computation.4 | async-start | bytes 786432 | tf_op jit(solution)/shard_map/all_to_all | solution.py:122
  110.7 2.5 %fusion.11 = bf16[32,16,4,80]{3,0,2,1:T(8,128)(2,1)} fusion(bf16[32,16,4,80]{3,2,1,0:T(4,128)(2,1)} %reshape.99, f32[16,4,32]{2,1,0:T(4,128)S(1)} %get-tuple-element.17, f32[16,4,32,32]{2,3,1,0:T(8,128)S(1)} %fusion.7), kind=kOutput, calls=%fused_computation.23 | convolution fusion | flops 10848287 | bytes 925696 | tf_op jit(solution)/shard_map/phij,jphd->iphd/dot_general | solution.py:61
  119.3 4.1 %all-to-all-start.7 = ((bf16[32,16,320]{2,1,0:T(8,128)(2,1)}), bf16[32,16,320]{2,1,0:T(8,128)(2,1)}, u32[]{:S(2)}, u32[]{:S(2)}) async-start(bf16[32,16,320]{2,1,0:T(8,128)(2,1)} %reshape.105), calls=%async_computation.7 | async-start | bytes 786432 | tf_op jit(solution)/shard_map/all_to_all | solution.py:121
  126.2 2.2 copy.76
  130.2 2.2 all-to-all-done.7
  135.5 2.3 reshape.104
  142.4 4.6 %copy.78 = f32[640,1280]{1,0:T(8,128)} copy(f32[640,1280]{0,1:T(8,128)} %pad_maximum_fusion) | data formatting | bytes 6553600
  149.9 72.6 %reduce-scatter.9.cloned.1.call-done = f32[80,1280]{1,0:T(8,128)} async-done(((f32[640,1280]{1,0:T(8,128)}), f32[80,1280]{1,0:T(8,128)}) %reduce-scatter.9.cloned.1.call-update) | async-done | bytes 409616
  (87 shorter events, 48.2 us)
Async XLA Ops:
  7.2 9.6 %copy-start = (bf16[640,3,320]{0,2,1:T(8,128)(2,1)S(1)}, bf16[640,3,320]{0,2,1:T(8,128)(2,1)}, u32[]{:S(2)}) copy-start(bf16[640,3,320]{0,2,1:T(8,128)(2,1)} %param.7) | copy-start | bytes 3686404
  7.2 9.4 %copy-start.11 = (bf16[8,64,640]{2,1,0:T(8,128)(2,1)S(1)}, bf16[8,64,640]{2,1,0:T(8,128)(2,1)}, u32[]{:S(2)}) copy-start(bf16[8,64,640]{2,1,0:T(8,128)(2,1)} %param.5) | copy-start | bytes 1966084
  10.0 18.0 %all-to-all-start.2 = ((bf16[8,64,320]{2,0,1:T(8,128)(2,1)}), bf16[8,64,320]{2,0,1:T(8,128)(2,1)S(1)}, u32[]{:S(2)}, u32[]{:S(2)}) async-start(bf16[8,64,320]{2,0,1:T(8,128)(2,1)} %copy.49), calls=%async_computation.2 | async-start | bytes 786432 | tf_op jit(solution)/shard_map/all_to_all | solution.py:115
  28.1 14.3 %all-to-all-start.3 = ((bf16[8,64,320]{2,0,1:T(8,128)(2,1)}), bf16[8,64,320]{2,0,1:T(8,128)(2,1)S(1)}, u32[]{:S(2)}, u32[]{:S(2)}) async-start(bf16[8,64,320]{2,0,1:T(8,128)(2,1)} %copy.51), calls=%async_computation.3 | async-start | bytes 786432 | tf_op jit(solution)/shard_map/all_to_all | solution.py:114
  32.5 26.7 %copy-start.12 = (f32[8,63]{1,0:T(8,128)S(1)}, f32[8,63]{1,0:T(8,128)}, u32[]{:S(2)}) copy-start(f32[8,63]{1,0:T(8,128)} %param.9) | copy-start | bytes 6052
  42.4 13.3 %all-to-all-start.1 = ((bf16[8,64,320]{2,0,1:T(8,128)(2,1)}), bf16[8,64,320]{2,0,1:T(8,128)(2,1)S(1)}, u32[]{:S(2)}, u32[]{:S(2)}) async-start(bf16[8,64,320]{2,0,1:T(8,128)(2,1)} %copy.43), calls=%async_computation.1 | async-start | bytes 786432 | tf_op jit(solution)/shard_map/all_to_all | solution.py:112
  55.7 14.3 %all-to-all-start = ((bf16[8,64,320]{2,0,1:T(8,128)(2,1)}), bf16[8,64,320]{2,0,1:T(8,128)(2,1)S(1)}, u32[]{:S(2)}, u32[]{:S(2)}) async-start(bf16[8,64,320]{2,0,1:T(8,128)(2,1)} %copy.41), calls=%async_computation | async-start | bytes 786432 | tf_op jit(solution)/shard_map/all_to_all | solution.py:113
  70.4 3.4 %copy-start.2 = (bf16[32,16,4,80]{3,2,1,0:T(4,128)(2,1)}, bf16[32,16,4,80]{3,2,1,0:T(4,128)(2,1)S(1)}, u32[]{:S(2)}) copy-start(bf16[32,16,4,80]{3,2,1,0:T(4,128)(2,1)S(1)} %reshape.96) | copy-start | bytes 983044
  78.7 14.4 %all-to-all-start.6 = ((bf16[32,16,320]{2,1,0:T(8,128)(2,1)}), bf16[32,16,320]{2,1,0:T(8,128)(2,1)}, u32[]{:S(2)}, u32[]{:S(2)}) async-start(bf16[32,16,320]{2,1,0:T(8,128)(2,1)} %reshape.102), calls=%async_computation.6 | async-start | bytes 786432 | tf_op jit(solution)/shard_map/all_to_all | solution.py:124
  83.7 3.0 %copy-start.3 = (bf16[32,16,4,80]{3,2,1,0:T(4,128)(2,1)S(1)}, bf16[32,16,4,80]{3,2,1,0:T(4,128)(2,1)}, u32[]{:S(2)}) copy-start(bf16[32,16,4,80]{3,2,1,0:T(4,128)(2,1)} %reshape.97) | copy-start | bytes 983044
  93.0 14.0 %all-to-all-start.5 = ((bf16[32,16,320]{2,1,0:T(8,128)(2,1)}), bf16[32,16,320]{2,1,0:T(8,128)(2,1)}, u32[]{:S(2)}, u32[]{:S(2)}) async-start(bf16[32,16,320]{2,1,0:T(8,128)(2,1)} %reshape.101), calls=%async_computation.5 | async-start | bytes 786432 | tf_op jit(solution)/shard_map/all_to_all | solution.py:123
  107.0 12.3 %all-to-all-start.4 = ((bf16[32,16,320]{2,1,0:T(8,128)(2,1)}), bf16[32,16,320]{2,1,0:T(8,128)(2,1)S(1)}, u32[]{:S(2)}, u32[]{:S(2)}) async-start(bf16[32,16,320]{2,1,0:T(8,128)(2,1)} %reshape.100), calls=%async_computation.4 | async-start | bytes 786432 | tf_op jit(solution)/shard_map/all_to_all | solution.py:122
  116.6 6.9 %copy-start.5 = (bf16[8,4,16,320]{3,2,1,0:T(8,128)(2,1)}, bf16[8,4,16,320]{3,2,1,0:T(8,128)(2,1)S(1)}, u32[]{:S(2)}) copy-start(bf16[8,4,16,320]{3,2,1,0:T(8,128)(2,1)S(1)} %copy.64) | copy-start | bytes 983044
  117.8 5.7 %copy-start.7 = (bf16[8,4,16,320]{3,2,1,0:T(8,128)(2,1)}, bf16[8,4,16,320]{3,2,1,0:T(8,128)(2,1)S(1)}, u32[]{:S(2)}) copy-start(bf16[8,4,16,320]{3,2,1,0:T(8,128)(2,1)S(1)} %copy.61) | copy-start | bytes 983044
  119.3 13.1 %all-to-all-start.7 = ((bf16[32,16,320]{2,1,0:T(8,128)(2,1)}), bf16[32,16,320]{2,1,0:T(8,128)(2,1)}, u32[]{:S(2)}, u32[]{:S(2)}) async-start(bf16[32,16,320]{2,1,0:T(8,128)(2,1)} %reshape.105), calls=%async_computation.7 | async-start | bytes 786432 | tf_op jit(solution)/shard_map/all_to_all | solution.py:121
  123.5 23.6 %reduce-scatter.7.cloned.1.call-start = ((), (), s32[]{:S(2)}) async-start(), calls=%async_computation.10 | async-start | bytes 983040
  123.6 0.8 copy-start.9
  130.1 4.1 %copy-start.6 = (bf16[8,4,16,320]{3,2,1,0:T(8,128)(2,1)S(1)}, bf16[8,4,16,320]{3,2,1,0:T(8,128)(2,1)}, u32[]{:S(2)}) copy-start(bf16[8,4,16,320]{3,2,1,0:T(8,128)(2,1)} %copy-done.5) | copy-start | bytes 983044
  130.1 4.1 %copy-start.8 = (bf16[8,4,16,320]{3,2,1,0:T(8,128)(2,1)S(1)}, bf16[8,4,16,320]{3,2,1,0:T(8,128)(2,1)}, u32[]{:S(2)}) copy-start(bf16[8,4,16,320]{3,2,1,0:T(8,128)(2,1)} %copy-done.7) | copy-start | bytes 983044
  130.1 4.1 %copy-start.10 = (bf16[8,4,16,320]{3,2,1,0:T(8,128)(2,1)S(1)}, bf16[8,4,16,320]{3,2,1,0:T(8,128)(2,1)}, u32[]{:S(2)}) copy-start(bf16[8,4,16,320]{3,2,1,0:T(8,128)(2,1)} %copy-done.9) | copy-start | bytes 983044
  130.1 92.4 %reduce-scatter.9.cloned.1.call-start = ((), (), s32[]{:S(2)}) async-start(), calls=%async_computation.11 | async-start | bytes 3686400
  137.8 1.8 copy-start.1
  147.0 1.9 copy-start.4
Sparse Core Ops, SparseCore 0:
  130.2 9.4 reduce-scatter.6
  147.2 75.3 reduce-scatter.8
where the time goes:
time: 235 us; the launch traced here: 233 us
  waiting for transfers between devices  107 us (46%)
  local copies, waits for them, and re-layouts  47.2 us (20%)
  starting transfers between devices  34.6 us (15%)
  matrix products  25.4 us (11%)
  between operations  14.4 us (6%)
  other arithmetic  4.71 us (2%)
    unnamed x4, waiting for transfers between devices  72.7 us
    unnamed x34, local copies, waits for them, and re-layouts  12.3 us
    all_to_all x1, waiting for transfers between devices, per_device(): lax.all_to_all(value_rows, 'tm', split_axis=1, concat_axis=0, tiled=True)  9.88 us
    all_to_all x1, waiting for transfers between devices, per_device(): lax.all_to_all(grad_attn, 'tm', split_axis=1, concat_axis=0, tiled=True)  9.01 us
    all_to_all x1, waiting for transfers between devices, per_device(): lax.all_to_all(query_rows, 'tm', split_axis=1, concat_axis=0, tiled=True)  8.82 us
    all_to_all x1, starting transfers between devices, per_device(): lax.all_to_all(grad_attn, 'tm', split_axis=1, concat_axis=0, tiled=True)  6.32 us
    gather x2, local copies, waits for them, and re-layouts, bias_table(): return bias_rows[:, offsets]  5.38 us
    all_to_all x1, starting transfers between devices, per_device(): lax.all_to_all(grad_value, 'tm', split_axis=0, concat_axis=1, tiled=True)  5.05 us
  transfers between devices with their start and end apart: 10, of which 8 were waited for; matrix products, arithmetic and copies ran while one was open for 26% of the time, Pallas kernels for 0%

commit v1 on v0

--- a/solution.py
+++ b/solution.py
@@ -5,6 +5,28 @@
 from jax.sharding import PartitionSpec as P
 
 H = 8
+
+
+def split_up(x, dim, length):
+    before, after = (x.shape[:dim], x.shape[dim + 1 :])
+    return jnp.moveaxis(x.reshape(*before, length, -1, *after), dim, 0)
+
+
+def laid_out(blocks, dim):
+    shape = list(blocks.shape[1:])
+    shape[dim] *= blocks.shape[0]
+    return jnp.moveaxis(blocks, 0, dim).reshape(shape)
+
+
+def sent_to_each(shard, axis, split_dim, concat_dim):
+    size, place = (lax.axis_size(axis), lax.axis_index(axis))
+    blocks = split_up(shard, split_dim, size)
+    outs = [blocks[place]]
+    for step in range(1, size):
+        sent = blocks[(place + step) % size]
+        outs.append(lax.ppermute(sent, axis, [(i, (i + step) % size) for i in range(size)]))
+    blocks = jnp.stack(outs)[(place - jnp.arange(size)) % size]
+    return laid_out(blocks, concat_dim)
 
 
 def positional(frame_pos, channels):
@@ -120,7 +142,7 @@
     attn_out, grad_query, grad_key, grad_value = (
         lax.all_to_all(attn_out, "tm", split_axis=0, concat_axis=1, tiled=True),
         lax.all_to_all(grad_query, "tm", split_axis=0, concat_axis=1, tiled=True),
-        lax.all_to_all(grad_key, "tm", split_axis=0, concat_axis=1, tiled=True),
+        sent_to_each(grad_key, "tm", 0, 1),
         lax.all_to_all(grad_value, "tm", split_axis=0, concat_axis=1, tiled=True),
     )
     grad_qkv = jnp.stack((grad_query, grad_key, grad_value), axis=2)

time: 235 us -> 237 us (level)
    all_to_all x1 -> x0, starting transfers between devices: 4.98 us -> none  [per_device(): lax.all_to_all(grad_key, 'tm', split_axis=0, concat_axis=1, tiled=True)]
    ppermute x0 -> x3, starting transfers between devices: none -> 4.95 us  [sent_to_each(): lax.ppermute(sent, axis, [(i, (i + step) % size) for i in range(size)])]
    all_to_all x1 -> x0, waiting for transfers between devices: 2.71 us -> none  [per_device(): lax.all_to_all(grad_key, 'tm', split_axis=0, concat_axis=1, tiled=True)]
    ppermute x0 -> x3, waiting for transfers between devices: none -> 2.69 us  [sent_to_each(): lax.ppermute(sent, axis, [(i, (i + step) % size) for i in range(size)])]
    unnamed x34 -> x36, local copies, waits for them, and re-layouts: 12.3 us -> 12.3 us
  transfers between devices with their start and end apart: 10 -> 12, of which waited for: 8 -> 7; matrix products, arithmetic and copies ran while one was open for 26% -> 26% of each run, Pallas kernels for 0% -> 0%
where the time goes in v1:
time: 237 us; the launch traced here: 235 us
  waiting for transfers between devices  105 us (44%)
  local copies, waits for them, and re-layouts  47.8 us (20%)
  starting transfers between devices  36.6 us (15%)
  matrix products  24.5 us (10%)
  between operations  14.5 us (6%)
  other arithmetic  6.43 us (3%)
    unnamed x4, waiting for transfers between devices  73.6 us
    unnamed x36, local copies, waits for them, and re-layouts  12.3 us
    all_to_all x1, waiting for transfers between devices, per_device(): lax.all_to_all(value_rows, 'tm', split_axis=1, concat_axis=0, tiled=True)  9.87 us
    all_to_all x1, waiting for transfers between devices, per_device(): lax.all_to_all(grad_attn, 'tm', split_axis=1, concat_axis=0, tiled=True)  9 us
    all_to_all x1, waiting for transfers between devices, per_device(): lax.all_to_all(query_rows, 'tm', split_axis=1, concat_axis=0, tiled=True)  8.83 us
    all_to_all x1, starting transfers between devices, per_device(): lax.all_to_all(grad_attn, 'tm', split_axis=1, concat_axis=0, tiled=True)  6.32 us
    gather x2, local copies, waits for them, and re-layouts, bias_table(): return bias_rows[:, offsets]  5.37 us
    all_to_all x1, starting transfers between devices, per_device(): lax.all_to_all(grad_query, 'tm', split_axis=0, concat_axis=1, tiled=True)  5.09 us
  transfers between devices with their start and end apart: 12, of which 7 were waited for; matrix products, arithmetic and copies ran while one was open for 26% of the time, Pallas kernels for 0%

profile of v1, /device:TPU:0, one launch (start us, length us, event | category | flops | bytes accessed | tf_op | source)
XLA Modules:
  0.0 235.2 jit_solution(5839023219279873113)
XLA Ops:
  10.0 6.3 %all-to-all-start.2 = ((bf16[8,64,320]{2,0,1:T(8,128)(2,1)}), bf16[8,64,320]{2,0,1:T(8,128)(2,1)S(1)}, u32[]{:S(2)}, u32[]{:S(2)}) async-start(bf16[8,64,320]{2,0,1:T(8,128)(2,1)} %copy.49), calls=%async_computation.2 | async-start | bytes 786432 | tf_op jit(solution)/shard_map/all_to_all | solution.py:137
  19.0 9.0 %all-to-all-done.2 = bf16[8,64,320]{2,0,1:T(8,128)(2,1)S(1)} async-done(((bf16[8,64,320]{2,0,1:T(8,128)(2,1)}), bf16[8,64,320]{2,0,1:T(8,128)(2,1)S(1)}, u32[]{:S(2)}, u32[]{:S(2)}) %all-to-all-start.2) | async-done | bytes 327712 | tf_op jit(solution)/shard_map/all_to_all | solution.py:137
  28.1 3.5 %all-to-all-start.3 = ((bf16[8,64,320]{2,0,1:T(8,128)(2,1)}), bf16[8,64,320]{2,0,1:T(8,128)(2,1)S(1)}, u32[]{:S(2)}, u32[]{:S(2)}) async-start(bf16[8,64,320]{2,0,1:T(8,128)(2,1)} %copy.51), calls=%async_computation.3 | async-start | bytes 786432 | tf_op jit(solution)/shard_map/all_to_all | solution.py:136
  32.5 9.9 %all-to-all-done.3 = bf16[8,64,320]{2,0,1:T(8,128)(2,1)S(1)} async-done(((bf16[8,64,320]{2,0,1:T(8,128)(2,1)}), bf16[8,64,320]{2,0,1:T(8,128)(2,1)S(1)}, u32[]{:S(2)}, u32[]{:S(2)}) %all-to-all-start.3) | async-done | bytes 327712 | tf_op jit(solution)/shard_map/all_to_all | solution.py:136
  42.4 3.5 %all-to-all-start.1 = ((bf16[8,64,320]{2,0,1:T(8,128)(2,1)}), bf16[8,64,320]{2,0,1:T(8,128)(2,1)S(1)}, u32[]{:S(2)}, u32[]{:S(2)}) async-start(bf16[8,64,320]{2,0,1:T(8,128)(2,1)} %copy.43), calls=%async_computation.1 | async-start | bytes 786432 | tf_op jit(solution)/shard_map/all_to_all | solution.py:134
  46.8 8.8 %all-to-all-done.1 = bf16[8,64,320]{2,0,1:T(8,128)(2,1)S(1)} async-done(((bf16[8,64,320]{2,0,1:T(8,128)(2,1)}), bf16[8,64,320]{2,0,1:T(8,128)(2,1)S(1)}, u32[]{:S(2)}, u32[]{:S(2)}) %all-to-all-start.1) | async-done | bytes 327712 | tf_op jit(solution)/shard_map/all_to_all | solution.py:134
  55.7 4.1 %all-to-all-start = ((bf16[8,64,320]{2,0,1:T(8,128)(2,1)}), bf16[8,64,320]{2,0,1:T(8,128)(2,1)}, u32[]{:S(2)}, u32[]{:S(2)}) async-start(bf16[8,64,320]{2,0,1:T(8,128)(2,1)} %copy.41), calls=%async_computation | async-start | bytes 786432 | tf_op jit(solution)/shard_map/all_to_all | solution.py:135
  60.0 4.0 %gather_fusion = f32[1024,4]{1,0:T(8,128)} fusion(f32[4,63]{0,1:T(8,128)S(1)} %copy.80, s32[1024]{0:T(1024)S(1)} %broadcast_clamp_fusion), kind=kCustom, calls=%fused_computation | custom fusion | bytes 36864 | tf_op jit(solution)/shard_map/gather | solution.py:46
  71.2 1.9 fusion.7
  74.3 2.5 %fusion.13 = bf16[32,16,4,80]{3,0,2,1:T(8,128)(2,1)} fusion(bf16[32,16,4,80]{3,2,1,0:T(4,128)(2,1)} %reshape.143, f32[16,4,32]{2,1,0:T(4,128)S(1)} %get-tuple-element.21, f32[16,4,32,32]{2,3,1,0:T(8,128)S(1)} %fusion.7), kind=kOutput, calls=%fused_computation.26 | convolution fusion | flops 10848287 | bytes 925696 | tf_op jit(solution)/shard_map/phij,iphd->jphd/dot_general | solution.py:97
  79.2 5.0 %all-to-all-start.5 = ((bf16[32,16,320]{2,1,0:T(8,128)(2,1)}), bf16[32,16,320]{2,1,0:T(8,128)(2,1)}, u32[]{:S(2)}, u32[]{:S(2)}) async-start(bf16[32,16,320]{2,1,0:T(8,128)(2,1)} %reshape.146), calls=%async_computation.5 | async-start | bytes 786432 | tf_op jit(solution)/shard_map/all_to_all | solution.py:146
  84.3 3.0 %fusion.27 = f32[16,4,32,32]{2,3,1,0:T(8,128)} fusion(bf16[32,16,4,80]{3,2,1,0:T(4,128)(2,1)} %reshape.144, bf16[32,16,4,80]{3,2,1,0:T(4,128)(2,1)} %reshape.143), kind=kOutput, calls=%fused_computation.40 | convolution fusion | flops 10485760 | bytes 917504 | tf_op jit(solution)/shard_map/iphd,jphd->phij/dot_general | solution.py:86
  87.3 3.7 %fusion.10 = bf16[32,16,4,80]{3,0,2,1:T(8,128)(2,1)} fusion(f32[16,4,32,32]{2,3,1,0:T(8,128)} %fusion.27, bf16[32,16,4,80]{3,2,1,0:T(4,128)(2,1)S(1)} %copy-done.3, f32[16,4,32,32]{2,3,1,0:T(8,128)} %get-tuple-element.22, f32[16,4,32]{2,1,0:T(4,128)S(1)} %get-tuple-element.21), kind=kOutput, calls=%fused_computation.23 | convolution fusion | flops 11110431 | bytes 1187840 | tf_op jit(solution)/shard_map/phij,jphd->iphd/dot_general | solution.py:91
  93.4 5.1 %all-to-all-start.4 = ((bf16[32,16,320]{2,1,0:T(8,128)(2,1)}), bf16[32,16,320]{2,1,0:T(8,128)(2,1)}, u32[]{:S(2)}, u32[]{:S(2)}) async-start(bf16[32,16,320]{2,1,0:T(8,128)(2,1)} %reshape.145), calls=%async_computation.4 | async-start | bytes 786432 | tf_op jit(solution)/shard_map/all_to_all | solution.py:144
  98.5 3.9 %fusion.12 = bf16[32,16,4,80]{3,0,2,1:T(8,128)(2,1)} fusion(f32[16,4,32,32]{2,3,1,0:T(8,128)} %fusion.27, bf16[32,16,4,80]{3,2,1,0:T(4,128)(2,1)} %copy-done.2, f32[16,4,32,32]{2,3,1,0:T(8,128)} %get-tuple-element.22, f32[16,4,32]{2,1,0:T(4,128)S(1)} %get-tuple-element.21), kind=kOutput, calls=%fused_computation.25 | convolution fusion | flops 11110431 | bytes 1187840 | tf_op jit(solution)/shard_map/phij,iphd->jphd/dot_general | solution.py:94
  106.6 3.8 %collective-permute-start.2 = (bf16[8,16,320]{2,1,0:T(8,128)(2,1)}, bf16[8,16,320]{2,1,0:T(8,128)(2,1)}, u32[]{:S(2)}, u32[]{:S(2)}) collective-permute-start(bf16[8,16,320]{2,1,0:T(8,128)(2,1)} %get-tuple-element.16), channel_id=1, source_target_pairs={{0,12},{4,0},{8,4},{12,8},{1,13},{5,1},{9,5},{13,9},{2,14},{6,2},{... | collective-permute-start | bytes 245768 | tf_op jit(solution)/shard_map/ppermute | solution.py:27
  114.6 2.7 %collective-permute-done.1 = bf16[8,16,320]{2,1,0:T(8,128)(2,1)} collective-permute-done((bf16[8,16,320]{2,1,0:T(8,128)(2,1)}, bf16[8,16,320]{2,1,0:T(8,128)(2,1)}, u32[]{:S(2)}, u32[]{:S(2)}) %collective-permute-start.1) | collective-permute-done | bytes 81952 | tf_op jit(solution)/shard_map/ppermute | solution.py:27
  120.4 4.1 %all-to-all-start.6 = ((bf16[32,16,320]{2,1,0:T(8,128)(2,1)}), bf16[32,16,320]{2,1,0:T(8,128)(2,1)}, u32[]{:S(2)}, u32[]{:S(2)}) async-start(bf16[32,16,320]{2,1,0:T(8,128)(2,1)} %reshape.149), calls=%async_computation.6 | async-start | bytes 786432 | tf_op jit(solution)/shard_map/all_to_all | solution.py:143
  126.4 1.9 fusion.8
  128.3 2.2 copy.76
  136.5 2.3 reshape.148
  141.7 1.9 pad_maximum_fusion
  143.6 4.6 %copy.78 = f32[640,1280]{1,0:T(8,128)} copy(f32[640,1280]{0,1:T(8,128)} %pad_maximum_fusion) | data formatting | bytes 6553600
  151.1 73.5 %reduce-scatter.9.cloned.1.call-done = f32[80,1280]{1,0:T(8,128)} async-done(((f32[640,1280]{1,0:T(8,128)}), f32[80,1280]{1,0:T(8,128)}) %reduce-scatter.9.cloned.1.call-update) | async-done | bytes 409616
  (98 shorter events, 49.5 us)
Async XLA Ops:
  7.2 9.6 %copy-start = (bf16[640,3,320]{0,2,1:T(8,128)(2,1)S(1)}, bf16[640,3,320]{0,2,1:T(8,128)(2,1)}, u32[]{:S(2)}) copy-start(bf16[640,3,320]{0,2,1:T(8,128)(2,1)} %param.7) | copy-start | bytes 3686404
  7.2 9.4 %copy-start.11 = (bf16[8,64,640]{2,1,0:T(8,128)(2,1)S(1)}, bf16[8,64,640]{2,1,0:T(8,128)(2,1)}, u32[]{:S(2)}) copy-start(bf16[8,64,640]{2,1,0:T(8,128)(2,1)} %param.5) | copy-start | bytes 1966084
  10.0 18.0 %all-to-all-start.2 = ((bf16[8,64,320]{2,0,1:T(8,128)(2,1)}), bf16[8,64,320]{2,0,1:T(8,128)(2,1)S(1)}, u32[]{:S(2)}, u32[]{:S(2)}) async-start(bf16[8,64,320]{2,0,1:T(8,128)(2,1)} %copy.49), calls=%async_computation.2 | async-start | bytes 786432 | tf_op jit(solution)/shard_map/all_to_all | solution.py:137
  28.1 14.3 %all-to-all-start.3 = ((bf16[8,64,320]{2,0,1:T(8,128)(2,1)}), bf16[8,64,320]{2,0,1:T(8,128)(2,1)S(1)}, u32[]{:S(2)}, u32[]{:S(2)}) async-start(bf16[8,64,320]{2,0,1:T(8,128)(2,1)} %copy.51), calls=%async_computation.3 | async-start | bytes 786432 | tf_op jit(solution)/shard_map/all_to_all | solution.py:136
  32.5 27.3 %copy-start.13 = (f32[8,63]{1,0:T(8,128)S(1)}, f32[8,63]{1,0:T(8,128)}, u32[]{:S(2)}) copy-start(f32[8,63]{1,0:T(8,128)} %param.9) | copy-start | bytes 6052
  42.4 13.3 %all-to-all-start.1 = ((bf16[8,64,320]{2,0,1:T(8,128)(2,1)}), bf16[8,64,320]{2,0,1:T(8,128)(2,1)S(1)}, u32[]{:S(2)}, u32[]{:S(2)}) async-start(bf16[8,64,320]{2,0,1:T(8,128)(2,1)} %copy.43), calls=%async_computation.1 | async-start | bytes 786432 | tf_op jit(solution)/shard_map/all_to_all | solution.py:134
  55.7 13.3 %all-to-all-start = ((bf16[8,64,320]{2,0,1:T(8,128)(2,1)}), bf16[8,64,320]{2,0,1:T(8,128)(2,1)}, u32[]{:S(2)}, u32[]{:S(2)}) async-start(bf16[8,64,320]{2,0,1:T(8,128)(2,1)} %copy.41), calls=%async_computation | async-start | bytes 786432 | tf_op jit(solution)/shard_map/all_to_all | solution.py:135
  68.8 4.3 %copy-start.2 = (bf16[32,16,4,80]{3,2,1,0:T(4,128)(2,1)}, bf16[32,16,4,80]{3,2,1,0:T(4,128)(2,1)S(1)}, u32[]{:S(2)}) copy-start(bf16[32,16,4,80]{3,2,1,0:T(4,128)(2,1)S(1)} %reshape.142) | copy-start | bytes 983044
  74.3 24.2 %copy-start.12 = (f32[16,4,32]{2,1,0:T(4,128)}, f32[16,4,32]{2,1,0:T(4,128)S(1)}, u32[]{:S(2)}) copy-start(f32[16,4,32]{2,1,0:T(4,128)S(1)} %get-tuple-element.21) | copy-start | bytes 24580
  79.2 14.2 %all-to-all-start.5 = ((bf16[32,16,320]{2,1,0:T(8,128)(2,1)}), bf16[32,16,320]{2,1,0:T(8,128)(2,1)}, u32[]{:S(2)}, u32[]{:S(2)}) async-start(bf16[32,16,320]{2,1,0:T(8,128)(2,1)} %reshape.146), calls=%async_computation.5 | async-start | bytes 786432 | tf_op jit(solution)/shard_map/all_to_all | solution.py:146
  84.3 3.0 %copy-start.3 = (bf16[32,16,4,80]{3,2,1,0:T(4,128)(2,1)S(1)}, bf16[32,16,4,80]{3,2,1,0:T(4,128)(2,1)}, u32[]{:S(2)}) copy-start(bf16[32,16,4,80]{3,2,1,0:T(4,128)(2,1)} %reshape.141) | copy-start | bytes 983044
  93.4 27.0 %all-to-all-start.4 = ((bf16[32,16,320]{2,1,0:T(8,128)(2,1)}), bf16[32,16,320]{2,1,0:T(8,128)(2,1)}, u32[]{:S(2)}, u32[]{:S(2)}) async-start(bf16[32,16,320]{2,1,0:T(8,128)(2,1)} %reshape.145), calls=%async_computation.4 | async-start | bytes 786432 | tf_op jit(solution)/shard_map/all_to_all | solution.py:144
  106.6 8.0 %collective-permute-start.2 = (bf16[8,16,320]{2,1,0:T(8,128)(2,1)}, bf16[8,16,320]{2,1,0:T(8,128)(2,1)}, u32[]{:S(2)}, u32[]{:S(2)}) collective-permute-start(bf16[8,16,320]{2,1,0:T(8,128)(2,1)} %get-tuple-element.16), channel_id=1, source_target_pairs={{0,12},{4,0},{8,4},{12,8},{1,13},{5,1},{9,5},{13,9},{2,14},{6,2},{... | collective-permute-start | bytes 245768 | tf_op jit(solution)/shard_map/ppermute | solution.py:27
  110.4 6.9 %collective-permute-start.1 = (bf16[8,16,320]{2,1,0:T(8,128)(2,1)}, bf16[8,16,320]{2,1,0:T(8,128)(2,1)}, u32[]{:S(2)}, u32[]{:S(2)}) collective-permute-start(bf16[8,16,320]{2,1,0:T(8,128)(2,1)} %get-tuple-element.17), channel_id=1, source_target_pairs={{0,8},{4,12},{8,0},{12,4},{1,9},{5,13},{9,1},{13,5},{2,10},{6,14},... | collective-permute-start | bytes 245768 | tf_op jit(solution)/shard_map/ppermute | solution.py:27
  110.4 6.9 %collective-permute-start = (bf16[8,16,320]{2,1,0:T(8,128)(2,1)}, bf16[8,16,320]{2,1,0:T(8,128)(2,1)}, u32[]{:S(2)}, u32[]{:S(2)}) collective-permute-start(bf16[8,16,320]{2,1,0:T(8,128)(2,1)} %get-tuple-element.18), channel_id=1, source_target_pairs={{0,4},{4,8},{8,12},{12,0},{1,5},{5,9},{9,13},{13,1},{2,6},{6,10},{... | collective-permute-start | bytes 245768 | tf_op jit(solution)/shard_map/ppermute | solution.py:27
  119.2 6.5 %copy-start.5 = (bf16[8,4,16,320]{3,2,1,0:T(8,128)(2,1)}, bf16[8,4,16,320]{3,2,1,0:T(8,128)(2,1)S(1)}, u32[]{:S(2)}) copy-start(bf16[8,4,16,320]{3,2,1,0:T(8,128)(2,1)S(1)} %copy.61) | copy-start | bytes 983044
  120.4 5.3 %copy-start.7 = (bf16[8,4,16,320]{3,2,1,0:T(8,128)(2,1)}, bf16[8,4,16,320]{3,2,1,0:T(8,128)(2,1)S(1)}, u32[]{:S(2)}) copy-start(bf16[8,4,16,320]{3,2,1,0:T(8,128)(2,1)S(1)} %copy.64) | copy-start | bytes 983044
  120.4 13.1 %all-to-all-start.6 = ((bf16[32,16,320]{2,1,0:T(8,128)(2,1)}), bf16[32,16,320]{2,1,0:T(8,128)(2,1)}, u32[]{:S(2)}, u32[]{:S(2)}) async-start(bf16[32,16,320]{2,1,0:T(8,128)(2,1)} %reshape.149), calls=%async_computation.6 | async-start | bytes 786432 | tf_op jit(solution)/shard_map/all_to_all | solution.py:143
  124.5 23.7 %reduce-scatter.7.cloned.1.call-start = ((), (), s32[]{:S(2)}) async-start(), calls=%async_computation.9 | async-start | bytes 983040
  132.1 3.1 %copy-start.6 = (bf16[8,4,16,320]{3,2,1,0:T(8,128)(2,1)S(1)}, bf16[8,4,16,320]{3,2,1,0:T(8,128)(2,1)}, u32[]{:S(2)}) copy-start(bf16[8,4,16,320]{3,2,1,0:T(8,128)(2,1)} %copy-done.5) | copy-start | bytes 983044
  132.1 3.1 %copy-start.8 = (bf16[8,4,16,320]{3,2,1,0:T(8,128)(2,1)S(1)}, bf16[8,4,16,320]{3,2,1,0:T(8,128)(2,1)}, u32[]{:S(2)}) copy-start(bf16[8,4,16,320]{3,2,1,0:T(8,128)(2,1)} %copy-done.7) | copy-start | bytes 983044
  132.1 3.1 %copy-start.10 = (bf16[8,4,16,320]{3,2,1,0:T(8,128)(2,1)S(1)}, bf16[8,4,16,320]{3,2,1,0:T(8,128)(2,1)}, u32[]{:S(2)}) copy-start(bf16[8,4,16,320]{3,2,1,0:T(8,128)(2,1)} %copy-done.9) | copy-start | bytes 983044
  132.2 92.4 %reduce-scatter.9.cloned.1.call-start = ((), (), s32[]{:S(2)}) async-start(), calls=%async_computation.10 | async-start | bytes 3686400
  148.2 1.9 copy-start.4
  (2 other events, 2.6 us)
Sparse Core Ops, SparseCore 0:
  132.3 9.4 reduce-scatter.6
  148.3 76.2 reduce-scatter.8
